TPU v7x, 256 devices: a whole 4x4x8 slice. The times are simulated.
256 devices in a mesh: member: 2 (over x_lo), space: 128 (over z, y, x_hi, core).
Axes of the slice: x: 4 (x_hi: 2, x_lo: 2; x = x_hi * 2 + x_lo), y: 4, z: 8, core: 2. Of those that a mesh axis runs over, the one named last changes fastest.
Arguments:
- params: float32 [256, 512, 1024], P('member', 'space'), may hold values from -2 to 2
- state: float32 [256, 512, 1024], P('member', 'space'), may hold values from -6 to 6
- regime: int32 [512, 1024], P('space'), may hold values from 0 to 7
- regime_coefs: float32 [8, 4], replicated, may hold values from 0.1 to 0.5
- observation_index: int32 [65536], P('space'), may hold values from 0 to 524287, as said below
- measured_values: float32 [65536], P('space'), may hold values from -6 to 6
- observation_spread: float32 [65536], P('space'), may hold values from 0.1 to 1
- observation_jitter: float32 [256, 65536], P('member', 'space'), may hold values from -6 to 6
Outputs:
- revised_log_diffusivity: float32 [256, 512, 1024], P('member', 'space')
- predicted_member_state: float32 [256, 512, 1024], P('member', 'space')
Inputs may be any that keep to these rules, and one draw needn't show every extreme that they name: `observation_index`: observation o lies in the strip of rows o // 512 * 4 up to (o // 512 + 1) * 4 - 1; the first observation of each strip sits on its first cell, the second on its last cell; cells may repeat.
All inputs are finite; a program needn't handle non-finite values.
Results may differ from a plain program's by a relative error of at most 0.015.
Values sent between devices are 32-bit elements; how exact they have to be, the bound alone decides.
No kernel may reach another device: no remote copies, remote signals or barrier semaphores. Data moves between devices by JAX's collectives and lax.ppermute only.
A program may use at most 64 MiB of HBM per device.

v0:
```python
import math
import jax
import jax.numpy as jnp
from jax import lax
from jax.sharding import PartitionSpec as P

time_step = 0.06


def with_halo(cells, sides, width):
    for axis, dim in sides:
        count = lax.axis_size(axis)
        ends = count - 1
        head = lax.slice_in_dim(cells, 0, width, axis=dim)
        tail = lax.slice_in_dim(cells, cells.shape[dim] - width, cells.shape[dim], axis=dim)
        cells = jnp.concatenate(
            [
                lax.ppermute(tail, axis, [(i, (i + 1) % count) for i in range(ends)]),
                cells,
                lax.ppermute(head, axis, [((i + 1) % count, i) for i in range(ends)]),
            ],
            axis=dim,
        )
    return cells


def coef_fields(regime, regime_coefs):
    levels = jnp.arange(regime_coefs.shape[0], dtype=jnp.int32)
    onehot = (regime[None, :, :] == levels[:, None, None]).astype(jnp.float32)
    return jnp.einsum("rd,rxy->dxy", regime_coefs, onehot, precision=lax.Precision.HIGHEST)


def advance(extended, rates, coefs):
    center = extended[..., 1:-1, :]
    widths = [(0, 0)] * (center.ndim - 1) + [(1, 1)]
    padded_cols = jnp.pad(center, widths)
    above = extended[..., :-2, :]
    below = extended[..., 2:, :]
    left_side = padded_cols[..., :-2]
    right_side = padded_cols[..., 2:]
    flow = coefs[0] * (above - center) + coefs[1] * (below - center)
    flow = flow + coefs[2] * (left_side - center) + coefs[3] * (right_side - center)
    return center + rates * flow


def body(
    params,
    state,
    regime,
    regime_coefs,
    observation_index,
    measured_values,
    observation_spread,
    observation_jitter,
):
    block_members = params.shape[0]
    strip_rows = params.shape[1]
    columns = params.shape[2]
    member_list = block_members * lax.axis_size("member")
    square_root_scale = math.sqrt(member_list - 1)
    coefs = coef_fields(regime, regime_coefs)
    rates = time_step * jnp.exp(params)
    current = state
    for repeat in range(2):
        extended = with_halo(current, (("space", 1),), 1)
        current = advance(extended, rates, coefs)
    param_anom = params / square_root_scale
    slab_local_index = observation_index - lax.axis_index("space") * (strip_rows * columns)
    flattened_grid = current.reshape(block_members, strip_rows * columns)
    local_predictions = jnp.take(flattened_grid, slab_local_index, axis=1)
    predicted_fields, noise_draws = (
        lax.all_gather(local_predictions, "member", axis=0, tiled=True),
        lax.all_gather(observation_jitter, "member", axis=0, tiled=True),
    )
    ensemble_mean_prediction = jnp.sum(predicted_fields, axis=0) / member_list
    member_departures = (predicted_fields - ensemble_mean_prediction[None, :]) / (
        observation_spread[None, :] * square_root_scale
    )
    observation_misfits = (
        measured_values[None, :] + observation_spread[None, :] * noise_draws - predicted_fields
    ) / observation_spread[None, :]
    stacked = jnp.concatenate([member_departures, observation_misfits], axis=0)
    own_start = lax.axis_index("member") * block_members
    own_anoms = lax.dynamic_slice_in_dim(member_departures, own_start, block_members, 0)
    block_rows = jnp.dot(
        own_anoms, stacked.T, precision=lax.Precision.HIGHEST, preferred_element_type=jnp.float32
    )
    block_rows = lax.psum(block_rows, "space")
    gram_full = lax.all_gather(block_rows, "member", axis=0, tiled=True)
    gram = gram_full[:, :member_list]
    cross = gram_full[:, member_list:]
    system = jnp.eye(member_list, dtype=jnp.float32) + gram
    factor = jnp.linalg.cholesky(system)
    mixing = jax.scipy.linalg.cho_solve((factor, True), cross)
    empty = jnp.zeros(params.shape, jnp.float32)
    piece = lax.all_gather(param_anom, "member", axis=0, tiled=True)
    weights = lax.dynamic_slice(mixing, (0, own_start), (piece.shape[0], block_members))
    update = empty + jnp.einsum("kj,kxy->jxy", weights, piece, precision=lax.Precision.HIGHEST)
    revised_log_diffusivity = params + update
    return (revised_log_diffusivity, current)


def solution(mesh):
    in_specs = (
        P("member", "space", None),
        P("member", "space", None),
        P("space", None),
        P(),
        P("space"),
        P("space"),
        P("space"),
        P("member", "space"),
    )
    out_specs = (P("member", "space", None), P("member", "space", None))
    return jax.shard_map(body, mesh=mesh, in_specs=in_specs, out_specs=out_specs, check_vma=False)
```

profile of v0, /device:TPU:2, one launch (start us, length us, event | category | flops | bytes accessed | tf_op | source)
XLA Modules:
  0.0 1354.0 jit_solution(15341635839725576717)
XLA Ops:
  8.1 2.8 copy.28
  10.9 1.3 copy-done.3
  12.2 1.0 fusion.53
  13.2 1.8 collective-permute-start
  15.0 1.3 collective-permute-start.1
  16.7 4.2 collective-permute-done.1
  20.9 5.7 fusion.5
  26.6 1.3 copy-done.2
  28.0 1.1 fusion.52
  29.0 13.7 %collective-permute-start.2 = (f32[128,1,1024]{2,0,1:T(8,128)}, f32[128,1,1024]{2,0,1:T(8,128)}, u32[]{:S(2)}, u32[]{:S(2)}) collective-permute-start(f32[128,1,1024]{2,0,1:T(8,128)} %get-tuple-element.28), channel_id=1, source_target_pairs={{0,1},{1,2},{2,3},{3,4},{4,5},{5,6},{6,7},{7,8},{8,9},{9,10},{10,1... | collective-permute-start | bytes 1572872 | tf_op jit(solution)/shard_map/ppermute | solution.py:18
  42.7 1.3 collective-permute-start.3
  44.2 15.5 %all_gather.13 = f32[256,512]{0,1:T(8,128)S(1)} all-gather(f32[128,512]{0,1:T(8,128)S(1)} %copy.30), channel_id=1, replica_groups=mesh['member'=2,'space'=128] {'member'}, dimensions={0}, use_global_device_ids=true | all-gather | bytes 786432 | tf_op jit(solution)/shard_map/all_gather | solution.py:73
  59.7 7.4 fusion.13
  67.1 2.9 copy.29
  70.0 2.6 gather_fusion
  72.8 9.4 all_gather.12
  82.7 2.5 fusion.26
  85.9 4.3 copy.37
  90.1 1177.7 %all-reduce.5.cloned.1.call-done = f32[128,512]{0,1:T(8,128)} async-done(((f32[128,512]{0,1:T(8,128)}), f32[128,512]{0,1:T(8,128)}) %all-reduce.5.cloned.1.call-update) | async-done | bytes 262160 | tf_op jit(solution)/shard_map/psum | solution.py:88
  1267.8 8.1 all_gather.14
  1276.2 11.7 cholesky.50
  1287.9 9.8 custom-call.18
  1298.2 11.7 cholesky.105
  1310.0 0.6 compare_reduce_fusion
  1310.6 0.6 compare_reduce_fusion.1
  1312.6 4.0 while.1
  1312.7 0.6 fusion.64
  1313.3 1.3 bitcast_dynamic-update-slice_fusion.2
  1315.2 1.3 bitcast_dynamic-update-slice_fusion.2
  1316.6 19.7 %custom-call.19 = f32[2,128,128]{1,2,0:T(8,128)S(1)} custom-call(f32[2,128,128]{2,1,0:T(8,128)S(1)} %get-tuple-element.9), custom_call_target="InvertDiagBlocksLowerTriangular" | custom-call | tf_op jit(solution)/shard_map/jit(_cho_solve)/triangular_solve | solution.py:94
  1338.2 5.7 copy_add_fusion
  1343.9 2.7 copy.36
  (58 shorter events, 5.1 us)
Async XLA Ops:
  8.0 8.3 copy-start
  8.0 1259.8 %all-reduce.5.cloned.1.call-start = ((), (), s32[]{:S(2)}) async-start(), calls=%async_computation | async-start | bytes 524288 | tf_op jit(solution)/shard_map/psum | solution.py:88
  8.1 8.3 copy-start.5
  10.9 1.3 copy-start.3
  12.2 8.7 copy-start.1
  13.2 3.5 collective-permute-start
  15.0 5.9 collective-permute-start.1
  26.6 1.3 copy-start.2
  28.0 16.1 %copy-start.7 = (s32[512]{0:T(512)S(1)}, s32[512]{0:T(512)}, u32[]{:S(2)}) copy-start(s32[512]{0:T(512)} %param.12) | copy-start | bytes 6148
  28.0 16.1 %copy-start.4 = (f32[128,512]{1,0:T(8,128)S(1)}, f32[128,512]{1,0:T(8,128)}, u32[]{:S(2)}) copy-start(f32[128,512]{1,0:T(8,128)} %param.15) | copy-start | bytes 786436
  28.0 31.7 %copy-start.6 = (f32[512]{0:T(512)S(1)}, f32[512]{0:T(512)}, u32[]{:S(2)}) copy-start(f32[512]{0:T(512)} %param.14) | copy-start | bytes 6148
  29.0 30.6 %collective-permute-start.2 = (f32[128,1,1024]{2,0,1:T(8,128)}, f32[128,1,1024]{2,0,1:T(8,128)}, u32[]{:S(2)}, u32[]{:S(2)}) collective-permute-start(f32[128,1,1024]{2,0,1:T(8,128)} %get-tuple-element.28), channel_id=1, source_target_pairs={{0,1},{1,2},{2,3},{3,4},{4,5},{5,6},{6,7},{7,8},{8,9},{9,10},{10,1... | collective-permute-start | bytes 1572872 | tf_op jit(solution)/shard_map/ppermute | solution.py:18
  42.7 16.9 %collective-permute-start.3 = (f32[128,1,1024]{2,0,1:T(8,128)}, f32[128,1,1024]{2,0,1:T(8,128)}, u32[]{:S(2)}, u32[]{:S(2)}) collective-permute-start(f32[128,1,1024]{2,0,1:T(8,128)} %get-tuple-element.29), channel_id=1, source_target_pairs={{1,0},{2,1},{3,2},{4,3},{5,4},{6,5},{7,6},{8,7},{9,8},{10,9},{11,1... | collective-permute-start | bytes 1572872 | tf_op jit(solution)/shard_map/ppermute | solution.py:20
  70.0 12.3 copy-start.8
  85.3 1252.9 %all-gather.2.cloned.1.call-start = ((), (), s32[]{:S(2)}) async-start(), calls=%async_computation.1 | async-start | bytes 6291456 | tf_op jit(solution)/shard_map/all_gather | solution.py:96
Sparse Core Ops, SparseCore 0:
  85.4 1182.4 all-reduce.4
Sparse Core Ops, SparseCore 1:
  87.5 65.5 all-gather.1
where the time goes:
time: 1350 us
  waiting for transfers between devices  1180 us (87%)
  other arithmetic  68.1 us (5%)
  blocking collectives  32.9 us (2%)
  local copies, waits for them, and re-layouts  24.2 us (2%)
  starting transfers between devices  18.1 us (1%)
  between operations  17.1 us (1%)
    psum x1, waiting for transfers between devices, body(): block_rows = lax.psum(block_rows, 'space')  1180 us
    another operation x7, other arithmetic, body(): factor = jnp.linalg.cholesky(system)  34.6 us
  transfers between devices with their start and end apart: 6, of which 3 were waited for; matrix products, arithmetic and copies ran while one was open for 5% of the time, Pallas kernels for 0%

commit v1 on v0

--- a/solution.py
+++ b/solution.py
@@ -85,7 +85,8 @@
     block_rows = jnp.dot(
         own_anoms, stacked.T, precision=lax.Precision.HIGHEST, preferred_element_type=jnp.float32
     )
-    block_rows = lax.psum(block_rows, "space")
+    terms = lax.all_gather(block_rows, "space", axis=0, tiled=False)
+    block_rows = terms.sum(axis=0)
     gram_full = lax.all_gather(block_rows, "member", axis=0, tiled=True)
     gram = gram_full[:, :member_list]
     cross = gram_full[:, member_list:]

time: 1350 us -> 406 us (0.30)
  waiting for transfers between devices: 1180 us -> 216 us
    psum x1 -> x0, waiting for transfers between devices: 1180 us -> none  [body(): block_rows = lax.psum(block_rows, 'space')]
    all_gather x0 -> x1, waiting for transfers between devices: none -> 211 us  [body(): terms = lax.all_gather(block_rows, 'space', axis=0, tiled=False)]
  transfers between devices with their start and end apart: 6 -> 6, of which waited for: 3 -> 3; matrix products, arithmetic and copies ran while one was open for 5% -> 19% of each run, Pallas kernels for 0% -> 0%
where the time goes in v1:
time: 406 us; the launch traced here: 404 us
  waiting for transfers between devices  216 us (53%)
  other arithmetic  80.3 us (20%)
  blocking collectives  40.2 us (10%)
  local copies, waits for them, and re-layouts  24.3 us (6%)
  starting transfers between devices  18.1 us (4%)
  between operations  15.6 us (4%)
  matrix products  9.79 us (2%)
    all_gather x1, waiting for transfers between devices, body(): terms = lax.all_gather(block_rows, 'space', axis=0, tiled=False)  211 us
    another operation x7, other arithmetic, body(): factor = jnp.linalg.cholesky(system)  34.6 us
    another operation x3, other arithmetic, body(): mixing = jax.scipy.linalg.cho_solve((factor, True), cross)  19.7 us
    all_gather x1, blocking collectives, body(): lax.all_gather(observation_jitter, 'member', axis=0, tiled=True)  15.5 us
    ppermute x2, starting transfers between devices, with_halo(): lax.ppermute(tail, axis, [(i, (i + 1) % count) for i in range(ends)])  15.5 us
    all_gather x1, blocking collectives, body(): gram_full = lax.all_gather(block_rows, 'member', axis=0, tiled=True)  15.4 us
    add x2, other arithmetic, advance(): return center + rates * flow  13 us
    unnamed x26, local copies, waits for them, and re-layouts  12.6 us
  transfers between devices with their start and end apart: 6, of which 3 were waited for; matrix products, arithmetic and copies ran while one was open for 19% of the time, Pallas kernels for 0%

profile of v1, /device:TPU:2, one launch (start us, length us, event | category | flops | bytes accessed | tf_op | source)
XLA Modules:
  0.0 404.2 jit_solution(10693556592101273321)
XLA Ops:
  7.2 2.8 copy.27
  10.1 1.3 copy-done.4
  11.4 1.0 fusion.53
  12.4 1.8 collective-permute-start
  14.2 1.3 collective-permute-start.1
  15.9 4.2 %collective-permute-done.1 = f32[128,1,1024]{2,0,1:T(8,128)S(1)} collective-permute-done((f32[128,1,1024]{2,0,1:T(8,128)}, f32[128,1,1024]{2,0,1:T(8,128)S(1)}, u32[]{:S(2)}, u32[]{:S(2)}) %collective-permute-start.1) | collective-permute-done | bytes 524320 | tf_op jit(solution)/shard_map/ppermute | solution.py:20
  20.1 5.7 %fusion.5 = f32[128,4,1024]{2,0,1:T(8,128)S(1)} fusion(f32[128,4,1024]{2,0,1:T(8,128)} %copy-done.4, f32[128,1,1024]{2,0,1:T(8,128)S(1)} %collective-permute-done.1, f32[128,1,1024]{2,0,1:T(8,128)S(1)} %collective-permute-done, f32[128,4,1024]{2,1,0:T(4,128)S(1)} %copy-done.2, f32[4,1024]{1,0:T(4,128)S(1)} %get-tuple-element.44, ...), kind=kLoop, calls=%fused_computation.12 | loop fusion | flops 8388608 | bytes 7405568 | tf_op jit(solution)/shard_map/add | solution.py:43
  25.8 1.3 copy-done.3
  27.2 1.1 fusion.52
  28.2 13.7 %collective-permute-start.2 = (f32[128,1,1024]{2,0,1:T(8,128)}, f32[128,1,1024]{2,0,1:T(8,128)}, u32[]{:S(2)}, u32[]{:S(2)}) collective-permute-start(f32[128,1,1024]{2,0,1:T(8,128)} %get-tuple-element.28), channel_id=1, source_target_pairs={{0,1},{1,2},{2,3},{3,4},{4,5},{5,6},{6,7},{7,8},{8,9},{9,10},{10,1... | collective-permute-start | bytes 1572872 | tf_op jit(solution)/shard_map/ppermute | solution.py:18
  41.9 1.3 collective-permute-start.3
  43.4 15.5 %all_gather.19 = f32[256,512]{0,1:T(8,128)S(1)} all-gather(f32[128,512]{0,1:T(8,128)S(1)} %copy.29), channel_id=1, replica_groups=mesh['member'=2,'space'=128] {'member'}, dimensions={0}, use_global_device_ids=true | all-gather | bytes 786432 | tf_op jit(solution)/shard_map/all_gather | solution.py:73
  58.9 7.3 %fusion.13 = (f32[128,4,1024]{2,0,1:T(8,128)}, f32[128,4,1024]{2,0,1:T(8,128)}) fusion(f32[128,4,1024]{2,0,1:T(8,128)} %copy-done.3, f32[128,1,1024]{2,0,1:T(8,128)} %collective-permute-done.3, f32[128,1,1024]{2,0,1:T(8,128)} %collective-permute-done.2, f32[128,4,1024]{2,1,0:T(4,128)S(1)} %copy-done.2, f32[4,1024]{1,0:T(4,128)S(1)} %get-tuple-element.44, ...), kind=kLoop, calls=%fused_computation.20 | loop fusion | flops 8912896 | bytes 9502720 | tf_op jit(solution)/shard_map/add | solution.py:43
  66.1 2.9 copy.28
  69.0 2.6 gather_fusion
  71.8 9.4 %all_gather.18 = f32[256,512]{0,1:T(8,128)S(1)} all-gather(f32[128,512]{0,1:T(8,128)S(1)} %select_bitcast_fusion), channel_id=1, replica_groups=mesh['member'=2,'space'=128] {'member'}, dimensions={0}, use_global_device_ids=true | all-gather | bytes 786432 | tf_op jit(solution)/shard_map/all_gather | solution.py:72
  81.7 1.5 fusion.26
  83.4 0.7 all-gather.4.cloned.1.call-update
  84.1 4.3 %copy.36 = f32[128,4,1024]{2,1,0:T(4,128)} copy(f32[128,4,1024]{2,0,1:T(8,128)} %get-tuple-element.26) | data formatting | bytes 4194304
  88.3 210.5 %all-gather.6.cloned.1.call-done = f32[16384,512]{1,0:T(8,128)} async-done(((f32[128,512]{1,0:T(8,128)}), f32[16384,512]{1,0:T(8,128)}) %all-gather.6.cloned.1.call-update) | async-done | bytes 33554448 | tf_op jit(solution)/shard_map/all_gather | solution.py:88
  298.8 12.3 %reduce_sum.19 = f32[128,512]{1,0:T(8,128)S(1)} reduce(f32[128,128,512]{2,1,0:T(8,128)} %bitcast.57, f32[]{:T(128)} %constant.118.clone.1), dimensions={0}, to_apply=%region_1.2 | reduce | flops 8323072 | bytes 33816580 | tf_op jit(solution)/shard_map/reduce_sum | solution.py:89
  311.3 15.4 %all_gather.22 = f32[256,512]{0,1:T(8,128)S(1)} all-gather(f32[128,512]{0,1:T(8,128)S(1)} %copy.30), channel_id=1, replica_groups=mesh['member'=2,'space'=128] {'member'}, dimensions={0}, use_global_device_ids=true | all-gather | bytes 786432 | tf_op jit(solution)/shard_map/all_gather | solution.py:90
  326.9 11.7 %cholesky.50 = f32[128,128]{1,0:T(8,128)S(1)} custom-call(f32[128,128]{1,0:T(8,128)S(1)} %cholesky.118), custom_call_target="Cholesky" | custom-call | tf_op jit(solution)/shard_map/jit(cholesky)/cholesky | solution.py:94
  338.7 9.8 %custom-call.18 = f32[1,128,128]{1,2,0:T(8,128)S(1)} custom-call(f32[1,128,128]{2,1,0:T(8,128)S(1)} %get-tuple-element.37), custom_call_target="InvertDiagBlocksLowerTriangular" | custom-call | tf_op jit(solution)/shard_map/jit(cholesky)/cholesky | solution.py:94
  348.9 11.7 %cholesky.105 = f32[128,128]{1,0:T(8,128)S(1)} custom-call(f32[128,128]{1,0:T(8,128)S(1)} %convolution_subtract_fusion.2), custom_call_target="Cholesky" | custom-call | tf_op jit(solution)/shard_map/jit(cholesky)/cholesky | solution.py:94
  360.7 0.6 compare_reduce_fusion
  363.3 4.0 while.1
  364.1 1.3 bitcast_dynamic-update-slice_fusion.2
  366.0 1.3 bitcast_dynamic-update-slice_fusion.2
  367.3 19.7 %custom-call.19 = f32[2,128,128]{1,2,0:T(8,128)S(1)} custom-call(f32[2,128,128]{2,1,0:T(8,128)S(1)} %get-tuple-element.9), custom_call_target="InvertDiagBlocksLowerTriangular" | custom-call | tf_op jit(solution)/shard_map/jit(_cho_solve)/triangular_solve | solution.py:95
  388.9 5.7 %copy_add_fusion = f32[128,4,1024]{2,0,1:T(8,128)S(1)} fusion(f32[128,4,1024]{2,1,0:T(4,128)S(1)} %copy-done.2, f32[256,4,1024]{2,0,1:T(8,128)} %all-gather.4.cloned.1.call-done, s32[]{:T(128)S(6)} %select_n.19, f32[128,256]{1,0:T(8,128)S(1)} %fusion.41, f32[128,256]{1,0:T(8,128)S(1)} %fusion.42), kind=kOutput, calls=%fused_computation.39 | convolution fusion | flops 1611169792 | bytes 8650756 | tf_op jit(solution)/shard_map/kj,kxy->jxy/dot_general | solution.py:99
  394.6 2.7 copy.35
  (62 shorter events, 5.9 us)
Async XLA Ops:
  7.2 8.3 %copy-start = (f32[8,4]{0,1:T(4,128)S(1)}, f32[8,4]{0,1:T(4,128)}, u32[]{:S(2)}) copy-start(f32[8,4]{0,1:T(4,128)} %param.11) | copy-start | bytes 388
  7.2 291.7 %all-gather.6.cloned.1.call-start = ((), (), s32[]{:S(2)}) async-start(), calls=%async_computation.1 | async-start | bytes 33816576 | tf_op jit(solution)/shard_map/all_gather | solution.py:88
  7.2 8.3 %copy-start.6 = (s32[4,1024]{1,0:T(4,128)S(1)}, s32[4,1024]{1,0:T(4,128)}, u32[]{:S(2)}) copy-start(s32[4,1024]{1,0:T(4,128)} %param.10) | copy-start | bytes 49156
  10.1 1.3 copy-start.4
  11.4 8.7 %copy-start.2 = (f32[128,4,1024]{2,1,0:T(4,128)S(1)}, f32[128,4,1024]{2,1,0:T(4,128)}, u32[]{:S(2)}) copy-start(f32[128,4,1024]{2,1,0:T(4,128)} %param.8) | copy-start | bytes 6291460
  12.4 3.5 collective-permute-start
  14.2 5.9 %collective-permute-start.1 = (f32[128,1,1024]{2,0,1:T(8,128)}, f32[128,1,1024]{2,0,1:T(8,128)S(1)}, u32[]{:S(2)}, u32[]{:S(2)}) collective-permute-start(f32[128,1,1024]{2,0,1:T(8,128)} %get-tuple-element.31), channel_id=1, source_target_pairs={{1,0},{2,1},{3,2},{4,3},{5,4},{6,5},{7,6},{8,7},{9,8},{10,9},{11,1... | collective-permute-start | bytes 1572872 | tf_op jit(solution)/shard_map/ppermute | solution.py:20
  25.8 1.3 copy-start.3
  27.2 16.1 %copy-start.8 = (s32[512]{0:T(512)S(1)}, s32[512]{0:T(512)}, u32[]{:S(2)}) copy-start(s32[512]{0:T(512)} %param.12) | copy-start | bytes 6148
  27.2 16.1 %copy-start.5 = (f32[128,512]{1,0:T(8,128)S(1)}, f32[128,512]{1,0:T(8,128)}, u32[]{:S(2)}) copy-start(f32[128,512]{1,0:T(8,128)} %param.15) | copy-start | bytes 786436
  27.2 31.7 %copy-start.7 = (f32[512]{0:T(512)S(1)}, f32[512]{0:T(512)}, u32[]{:S(2)}) copy-start(f32[512]{0:T(512)} %param.14) | copy-start | bytes 6148
  28.2 30.6 %collective-permute-start.2 = (f32[128,1,1024]{2,0,1:T(8,128)}, f32[128,1,1024]{2,0,1:T(8,128)}, u32[]{:S(2)}, u32[]{:S(2)}) collective-permute-start(f32[128,1,1024]{2,0,1:T(8,128)} %get-tuple-element.28), channel_id=1, source_target_pairs={{0,1},{1,2},{2,3},{3,4},{4,5},{5,6},{6,7},{7,8},{8,9},{9,10},{10,1... | collective-permute-start | bytes 1572872 | tf_op jit(solution)/shard_map/ppermute | solution.py:18
  41.9 16.9 %collective-permute-start.3 = (f32[128,1,1024]{2,0,1:T(8,128)}, f32[128,1,1024]{2,0,1:T(8,128)}, u32[]{:S(2)}, u32[]{:S(2)}) collective-permute-start(f32[128,1,1024]{2,0,1:T(8,128)} %get-tuple-element.29), channel_id=1, source_target_pairs={{1,0},{2,1},{3,2},{4,3},{5,4},{6,5},{7,6},{8,7},{9,8},{10,9},{11,1... | collective-permute-start | bytes 1572872 | tf_op jit(solution)/shard_map/ppermute | solution.py:20
  69.0 12.3 %copy-start.9 = (f32[512]{0:T(512)S(1)}, f32[512]{0:T(512)}, u32[]{:S(2)}) copy-start(f32[512]{0:T(512)} %param.13) | copy-start | bytes 6148
  83.3 305.6 %all-gather.4.cloned.1.call-start = ((), (), s32[]{:S(2)}) async-start(), calls=%async_computation | async-start | bytes 6291456 | tf_op jit(solution)/shard_map/all_gather | solution.py:97
  388.9 8.4 %copy-start.1 = (f32[8,4]{0,1:T(4,128)S(1)}, f32[8,4]{0,1:T(4,128)}, u32[]{:S(2)}) copy-start(f32[8,4]{0,1:T(4,128)} %param.11) | copy-start | bytes 388
Sparse Core Ops, SparseCore 0:
  83.4 215.3 all-gather.5
  300.6 63.9 all-gather.3
